TPU v7x, 32 devices: a whole 2x2x4 slice. The times are simulated.
32 devices in a mesh: grp: 4 (over y, x), own: 8 (over z, core).
Axes of the slice: x: 2, y: 2, z: 4, core: 2. Of those that a mesh axis runs over, the one named last changes fastest.
Arguments:
- embeddings: float32 [24576, 768], P(('grp', 'own')), may hold values from -64 to 64
- cluster_ids: int32 [24576], P(('grp', 'own')), may hold values from 0 to 127, as said below
- owner_map: int32 [128], replicated, may hold values from 0 to 7, as said below
- source_order: int32 [24576], P(('grp', 'own')), may hold values from 0 to 767, as said below
Outputs:
- dup_score: float32 [24576], P(('grp', 'own'))
- centroids: float32 [128, 768], P('own')
Inputs may be any that keep to these rules, and one draw needn't show every extreme that they name: `owner_map`: every owner index is given to exactly 16 clusters. `cluster_ids`: within the 768 rows of one device, at most 192 rows have clusters of one owner index; in every draw some owner index receives exactly 192 rows from every device, and every device sends exactly 192 rows to some owner index. Cluster sizes are uneven and some clusters may be empty. `source_order`: each aligned block of 768 entries is a permutation of 0 to 767.
All inputs are finite; a program needn't handle non-finite values.
Results may differ from a plain program's by a relative error of at most 0.0003.
Values sent between devices are 32-bit elements; how exact they have to be, the bound alone decides.
No kernel may reach another device: no remote copies, remote signals or barrier semaphores. Data moves between devices by JAX's collectives and lax.ppermute only.
A program may use at most 128 MiB of HBM per device.

v0:
```python
import jax
import jax.numpy as jnp
from jax import lax
from jax.sharding import PartitionSpec as P

CL_OWN = 16
sharpness = 6.0


def passed_along(value, axis, steps):
    count = lax.axis_size(axis)
    pairs = [(source, (source + steps) % count) for source in range(count)]
    return lax.ppermute(value, axis, pairs)


def unit_rows(embeddings):
    squares = jnp.sum(embeddings * embeddings, axis=1, keepdims=True)
    return embeddings * lax.rsqrt(squares + 1e-06)


def owner_positions(owner_map):
    cluster_index = jnp.arange(owner_map.shape[0], dtype=jnp.int32)
    same_owner = owner_map[:, None] == owner_map[None, :]
    earlier = cluster_index[None, :] < cluster_index[:, None]
    before = jnp.sum((same_owner & earlier).astype(jnp.int32), axis=1)
    return owner_map * CL_OWN + before


def masked_weights(left_rows, left_ids, right_rows, right_ids):
    scores = jnp.einsum(
        "id,jd->ij",
        left_rows,
        right_rows,
        preferred_element_type=jnp.float32,
        precision=lax.Precision.HIGHEST,
    )
    linked = (left_ids[:, None] == right_ids[None, :]) & (left_ids[:, None] >= 0)
    return jnp.where(linked, jnp.exp(sharpness * (scores - 1.0)), 0.0)


def tile_sums(left_rows, left_ids, right_rows, right_ids, with_columns):
    right_count = right_rows.shape[0]
    block_rows = 512
    block_count = right_count // block_rows
    right_blocks = right_rows.reshape(block_count, block_rows, right_rows.shape[1])
    id_blocks = right_ids.reshape(block_count, block_rows)

    def one_block(row_total, block_pair):
        weights = masked_weights(left_rows, left_ids, block_pair[0], block_pair[1])
        column_part = jnp.sum(weights, axis=0) if with_columns else None
        return (row_total + jnp.sum(weights, axis=1), column_part)

    row_sums, column_sums = lax.scan(
        one_block, jnp.zeros((left_rows.shape[0],), jnp.float32), (right_blocks, id_blocks)
    )
    if with_columns:
        column_sums = column_sums.reshape(right_count)
    return (row_sums, column_sums)


def local(embeddings, cluster_ids, owner_map, source_order):
    row_count, feature_width = embeddings.shape
    owner_count = lax.axis_size("own")
    capacity = 2 * row_count // owner_count
    slot_count = owner_count * capacity
    cluster_count = owner_map.shape[0]
    unit_embed = unit_rows(embeddings)
    cluster_index = jnp.arange(cluster_count, dtype=jnp.int32)
    cluster_match = cluster_ids[:, None] == cluster_index[None, :]
    row_owner = jnp.sum(jnp.where(cluster_match, owner_map[None, :], 0), axis=1)
    owner_hot = (row_owner[:, None] == jnp.arange(owner_count, dtype=jnp.int32)[None, :]).astype(
        jnp.int32
    )
    rank_index = jnp.sum(jnp.cumsum(owner_hot, axis=0) * owner_hot, axis=1) - 1
    slot_index = row_owner * capacity + rank_index
    send_rows = jnp.zeros((slot_count, feature_width), jnp.float32).at[slot_index].set(unit_embed)
    send_ids = jnp.full((slot_count,), -1, jnp.int32).at[slot_index].set(cluster_ids)
    held_rows, held_ids = (
        lax.all_to_all(
            send_rows.reshape(owner_count, capacity, feature_width),
            "own",
            split_axis=0,
            concat_axis=0,
            tiled=True,
        ),
        lax.all_to_all(
            send_ids.reshape(owner_count, capacity), "own", split_axis=0, concat_axis=0, tiled=True
        ),
    )
    held_rows = held_rows.reshape(slot_count, feature_width)
    held_ids = held_ids.reshape(slot_count)
    group_count = lax.axis_size("grp")
    dup_mass, column_sums = tile_sums(held_rows, held_ids, held_rows, held_ids, False)
    for offset in range(1, group_count // 2 + 1):
        far_rows, far_ids = passed_along((held_rows, held_ids), "grp", -offset)
        returning = offset < group_count - offset
        row_sums, column_sums = tile_sums(held_rows, held_ids, far_rows, far_ids, returning)
        dup_mass = dup_mass + row_sums
        if returning:
            dup_mass = dup_mass + passed_along(column_sums, "grp", offset)
    returned = lax.all_to_all(
        dup_mass.reshape(owner_count, capacity), "own", split_axis=0, concat_axis=0, tiled=True
    )
    row_score = jnp.log(returned.reshape(slot_count)[slot_index])
    dup_score = jnp.zeros((row_count,), jnp.float32).at[source_order].set(row_score)
    position = owner_positions(owner_map)
    position_index = jnp.arange(cluster_count, dtype=jnp.int32)
    ordered = jnp.sum(
        jnp.where(position[None, :] == position_index[:, None], cluster_index[None, :], 0), axis=1
    )
    cluster_hot = (cluster_ids[:, None] == ordered[None, :]).astype(jnp.float32)
    cluster_terms = lax.dot_general(
        cluster_hot,
        unit_embed,
        (((0,), (0,)), ((), ())),
        preferred_element_type=jnp.float32,
        precision=lax.Precision.HIGHEST,
    )
    partial_value = lax.psum_scatter(cluster_terms, "own", scatter_dimension=0, tiled=True)
    cluster_sums = lax.psum(partial_value, "grp")
    centroids = cluster_sums * lax.rsqrt(
        jnp.mean(cluster_sums * cluster_sums, axis=1, keepdims=True) + 1e-06
    )
    return (dup_score, centroids)


def solution(mesh):
    placed = (P(("grp", "own"), None), P(("grp", "own")), P(), P(("grp", "own")))
    return jax.shard_map(
        local,
        mesh=mesh,
        in_specs=placed,
        out_specs=(P(("grp", "own")), P("own", None)),
        check_vma=False,
    )
```

profile of v0, /device:TPU:0, one launch (start us, length us, event | category | flops | bytes accessed | tf_op | source)
XLA Modules:
  0.0 413.7 jit_solution(8130020601397739330)
XLA Ops:
  7.2 1.1 select_reduce_fusion
  8.3 1.7 reduce-window.6
  10.6 1.9 multiply_reduce_fusion
  12.6 9.8 %scatter_custom_fusion.1 = f32[1536,768]{1,0:T(8,128)} fusion(s32[768]{0:T(1024)S(1)} %fusion.42, f32[]{:T(128)} %constant.122.clone.1, f32[768,768]{1,0:T(8,128)S(1)} %copy-done, f32[768]{0:T(1024)S(1)} %add_rsqrt_fusion), kind=kCustom, calls=%fused_computation.40 | custom fusion | flops 589824 | bytes 7081988 | tf_op jit(solution)/shard_map/scatter | solution.py:76
  22.3 6.5 %all-to-all-start.1 = ((f32[8,192,768]{2,1,0:T(8,128)}), f32[8,192,768]{2,1,0:T(8,128)}, u32[]{:S(2)}, u32[]{:S(2)}) async-start(f32[8,192,768]{2,1,0:T(8,128)} %bitcast.91), calls=%async_computation.1 | async-start | bytes 9437184 | tf_op jit(solution)/shard_map/all_to_all | solution.py:79
  29.0 105.1 %all-to-all-done.1 = f32[8,192,768]{2,1,0:T(8,128)} async-done(((f32[8,192,768]{2,1,0:T(8,128)}), f32[8,192,768]{2,1,0:T(8,128)}, u32[]{:S(2)}, u32[]{:S(2)}) %all-to-all-start.1) | async-done | bytes 4718624 | tf_op jit(solution)/shard_map/all_to_all | solution.py:79
  134.1 2.4 collective-permute-start.1
  136.7 1.9 fusion.29
  138.6 3.4 scatter_custom_fusion
  142.0 0.7 all_to_all.17
  142.7 3.3 all-to-all-start
  146.1 5.5 %all-to-all-done = s32[8,1,192]{2,1,0:T(1,128)S(1)} async-done(((s32[8,1,192]{2,1,0:T(1,128)}), s32[8,1,192]{2,1,0:T(1,128)S(1)}, u32[]{:S(2)}, u32[]{:S(2)}) %all-to-all-start) | async-done | bytes 6176 | tf_op jit(solution)/shard_map/all_to_all | solution.py:86
  153.1 84.7 %collective-permute-done = s32[1536]{0:T(1024)S(1)} collective-permute-done((s32[1536]{0:T(1024)S(1)}, s32[1536]{0:T(1024)S(1)}, u32[]{:S(2)}, u32[]{:S(2)}) %collective-permute-start) | collective-permute-done | bytes 6176 | tf_op jit(solution)/shard_map/ppermute | solution.py:13
  237.8 18.5 %psum.7 = f32[16,768]{1,0:T(8,128)S(1)} all-reduce(f32[16,768]{1,0:T(8,128)} %reduce-scatter.2.cloned.1.call-done), channel_id=1, replica_groups=mesh['grp'=4,'own'=8] {'grp'}, use_global_device_ids=true, to_apply=%region_21.22 | all-reduce | flops 12288 | bytes 98304 | tf_op jit(solution)/shard_map/psum | solution.py:120
  257.0 33.5 %while.44 = (s32[]{:T(128)}, f32[1536]{0:T(1024)S(1)}, s32[8,192]{1,0:T(8,128)}, s32[3,512]{1,0:T(4,128)S(1)}, f32[3,512,768]{2,1,0:T(8,128)}, /*index=5*/f32[15...) while((s32[]{:T(128)}, f32[1536]{0:T(1024)S(1)}, s32[8,192]{1,0:T(8,128)}, ...), condition=%wide.wide.region_9.10_spmd.clone, body=%wide.wide.region_7.9_spmd.clone.sunk | while | flops 7252478976 | bytes 6338155 | solution.py:53
  257.0 11.5 %fusion.67 = f32[1536]{0:T(1024)S(1)} fusion(f32[1536,768]{1,0:T(8,128)} %get-tuple-element.653, f32[3,512,768]{2,1,0:T(8,128)} %get-tuple-element.652, s32[]{:T(128)} %get-tuple-element.639, pred[1536]{0:T(1024)(128)(4,1)S(1)} %broadcast_compare_fusion.9, s32[512]{0:T(512)S(1)} %bitcast.99, s32[1536]{0:T(1024)S(1)} %get-tuple-element.654), kind=kOutput, calls=%fused_computation.11.clone.clone.1 | convolution fusion | flops 7252474368 | bytes 6307840 | tf_op jit(solution)/shard_map/while/body/eval_jaxpr/id,jd->ij/dot_general | solution.py:30
  268.5 10.9 %fusion.67 = f32[1536]{0:T(1024)S(1)} fusion(f32[1536,768]{1,0:T(8,128)} %get-tuple-element.653, f32[3,512,768]{2,1,0:T(8,128)} %get-tuple-element.652, s32[]{:T(128)} %get-tuple-element.639, pred[1536]{0:T(1024)(128)(4,1)S(1)} %broadcast_compare_fusion.9, s32[512]{0:T(512)S(1)} %bitcast.99, s32[1536]{0:T(1024)S(1)} %get-tuple-element.654), kind=kOutput, calls=%fused_computation.11.clone.clone.1 | convolution fusion | flops 7252474368 | bytes 6307840 | tf_op jit(solution)/shard_map/while/body/eval_jaxpr/id,jd->ij/dot_general | solution.py:30
  279.5 10.9 %fusion.67 = f32[1536]{0:T(1024)S(1)} fusion(f32[1536,768]{1,0:T(8,128)} %get-tuple-element.653, f32[3,512,768]{2,1,0:T(8,128)} %get-tuple-element.652, s32[]{:T(128)} %get-tuple-element.639, pred[1536]{0:T(1024)(128)(4,1)S(1)} %broadcast_compare_fusion.9, s32[512]{0:T(512)S(1)} %bitcast.99, s32[1536]{0:T(1024)S(1)} %get-tuple-element.654), kind=kOutput, calls=%fused_computation.11.clone.clone.1 | convolution fusion | flops 7252474368 | bytes 6307840 | tf_op jit(solution)/shard_map/while/body/eval_jaxpr/id,jd->ij/dot_general | solution.py:30
  290.5 32.8 %while.45 = (s32[]{:T(128)}, f32[1536]{0:T(1024)S(1)}, f32[3,512]{1,0:T(4,128)S(1)}, s32[8,192]{1,0:T(8,128)}, s32[3,512]{1,0:T(4,128)S(1)}, /*index=5*/f32[3,51...) while((s32[]{:T(128)}, f32[1536]{0:T(1024)S(1)}, ...), condition=%wide.wide.region_13.14_spmd.clone, body=%wide.wide.region_10.13_spmd.clone.sunk | while | flops 7253264896 | bytes 6344311 | solution.py:53
  290.5 10.8 %fusion.69 = (f32[512]{0:T(512)S(1)}, f32[1536]{0:T(1024)S(1)}) fusion(f32[1536,768]{1,0:T(8,128)} %get-tuple-element.626, f32[3,512,768]{2,1,0:T(8,128)} %get-tuple-element.625, s32[]{:T(128)} %get-tuple-element.610, pred[1536]{0:T(1024)(128)(4,1)S(1)} %broadcast_compare_fusion.10, s32[512]{0:T(512)S(1)} %bitcast.98, ...), kind=kOutput, calls=%fused_computation.78.clone.clone.1 | convolution fusion | flops 7253260288 | bytes 6309888 | tf_op jit(solution)/shard_map/while/body/eval_jaxpr/id,jd->ij/dot_general | solution.py:30
  301.5 10.8 %fusion.69 = (f32[512]{0:T(512)S(1)}, f32[1536]{0:T(1024)S(1)}) fusion(f32[1536,768]{1,0:T(8,128)} %get-tuple-element.626, f32[3,512,768]{2,1,0:T(8,128)} %get-tuple-element.625, s32[]{:T(128)} %get-tuple-element.610, pred[1536]{0:T(1024)(128)(4,1)S(1)} %broadcast_compare_fusion.10, s32[512]{0:T(512)S(1)} %bitcast.98, ...), kind=kOutput, calls=%fused_computation.78.clone.clone.1 | convolution fusion | flops 7253260288 | bytes 6309888 | tf_op jit(solution)/shard_map/while/body/eval_jaxpr/id,jd->ij/dot_general | solution.py:30
  312.4 10.8 %fusion.69 = (f32[512]{0:T(512)S(1)}, f32[1536]{0:T(1024)S(1)}) fusion(f32[1536,768]{1,0:T(8,128)} %get-tuple-element.626, f32[3,512,768]{2,1,0:T(8,128)} %get-tuple-element.625, s32[]{:T(128)} %get-tuple-element.610, pred[1536]{0:T(1024)(128)(4,1)S(1)} %broadcast_compare_fusion.10, s32[512]{0:T(512)S(1)} %bitcast.98, ...), kind=kOutput, calls=%fused_computation.78.clone.clone.1 | convolution fusion | flops 7253260288 | bytes 6309888 | tf_op jit(solution)/shard_map/while/body/eval_jaxpr/id,jd->ij/dot_general | solution.py:30
  323.6 32.1 %collective-permute-done.4 = f32[1536,768]{1,0:T(8,128)} collective-permute-done((f32[1536,768]{1,0:T(8,128)}, f32[1536,768]{1,0:T(8,128)}, u32[]{:S(2)}, u32[]{:S(2)}) %collective-permute-start.4) | collective-permute-done | bytes 4718624 | tf_op jit(solution)/shard_map/ppermute | solution.py:13
  355.8 32.9 %while.46 = (s32[]{:T(128)}, f32[1536]{0:T(1024)S(1)}, s32[8,192]{1,0:T(8,128)}, s32[3,512]{1,0:T(4,128)S(1)}, f32[3,512,768]{2,1,0:T(8,128)}, /*index=5*/f32[15...) while((s32[]{:T(128)}, f32[1536]{0:T(1024)S(1)}, s32[8,192]{1,0:T(8,128)}, ...), condition=%wide.wide.region_16.17_spmd.clone, body=%wide.wide.region_14.16_spmd.clone.sunk | while | flops 7252478976 | bytes 6338155 | solution.py:53
  355.8 10.9 %fusion.72 = f32[1536]{0:T(1024)S(1)} fusion(f32[1536,768]{1,0:T(8,128)} %get-tuple-element.596, f32[3,512,768]{2,1,0:T(8,128)} %get-tuple-element.595, s32[]{:T(128)} %get-tuple-element.582, pred[1536]{0:T(1024)(128)(4,1)S(1)} %broadcast_compare_fusion.11, s32[512]{0:T(512)S(1)} %bitcast.100, s32[1536]{0:T(1024)S(1)} %get-tuple-element.597), kind=kOutput, calls=%fused_computation.34.clone.clone.1 | convolution fusion | flops 7252474368 | bytes 6307840 | tf_op jit(solution)/shard_map/while/body/eval_jaxpr/id,jd->ij/dot_general | solution.py:30
  366.7 10.9 %fusion.72 = f32[1536]{0:T(1024)S(1)} fusion(f32[1536,768]{1,0:T(8,128)} %get-tuple-element.596, f32[3,512,768]{2,1,0:T(8,128)} %get-tuple-element.595, s32[]{:T(128)} %get-tuple-element.582, pred[1536]{0:T(1024)(128)(4,1)S(1)} %broadcast_compare_fusion.11, s32[512]{0:T(512)S(1)} %bitcast.100, s32[1536]{0:T(1024)S(1)} %get-tuple-element.597), kind=kOutput, calls=%fused_computation.34.clone.clone.1 | convolution fusion | flops 7252474368 | bytes 6307840 | tf_op jit(solution)/shard_map/while/body/eval_jaxpr/id,jd->ij/dot_general | solution.py:30
  377.7 10.9 %fusion.72 = f32[1536]{0:T(1024)S(1)} fusion(f32[1536,768]{1,0:T(8,128)} %get-tuple-element.596, f32[3,512,768]{2,1,0:T(8,128)} %get-tuple-element.595, s32[]{:T(128)} %get-tuple-element.582, pred[1536]{0:T(1024)(128)(4,1)S(1)} %broadcast_compare_fusion.11, s32[512]{0:T(512)S(1)} %bitcast.100, s32[1536]{0:T(1024)S(1)} %get-tuple-element.597), kind=kOutput, calls=%fused_computation.34.clone.clone.1 | convolution fusion | flops 7252474368 | bytes 6307840 | tf_op jit(solution)/shard_map/while/body/eval_jaxpr/id,jd->ij/dot_general | solution.py:30
  389.4 3.4 all-to-all-start.2
  392.7 0.7 broadcast_multiply_fusion
  393.4 4.9 %all-to-all-done.2 = f32[8,1,192]{2,1,0:T(1,128)S(1)} async-done(((f32[8,1,192]{2,1,0:T(1,128)}), f32[8,1,192]{2,1,0:T(1,128)S(1)}, u32[]{:S(2)}, u32[]{:S(2)}) %all-to-all-start.2) | async-done | bytes 6176 | tf_op jit(solution)/shard_map/all_to_all | solution.py:101
  398.4 4.5 %gather_fusion = f32[768]{0:T(1024)S(1)} fusion(f32[1536]{0:T(1024)S(1)} %reshape.150, s32[1024]{0:T(1024)S(1)} %pad_clamp_fusion), kind=kCustom, calls=%fused_computation | custom fusion | bytes 9216 | tf_op jit(solution)/shard_map/gather | solution.py:104
  402.9 3.9 scatter_custom_fusion.2
  (85 shorter events, 4.5 us)
Async XLA Ops:
  7.2 5.4 %copy-start = (f32[768,768]{1,0:T(8,128)S(1)}, f32[768,768]{1,0:T(8,128)}, u32[]{:S(2)}) copy-start(f32[768,768]{1,0:T(8,128)} %param.10) | copy-start | bytes 7077892
  22.3 6.5 %copy-start.4 = (s32[128]{0:T(128)S(1)}, s32[128]{0:T(128)}, u32[]{:S(2)}) copy-start(s32[128]{0:T(128)} %param.12) | copy-start | bytes 1540
  22.3 114.4 %copy-start.2 = (s32[768]{0:T(1024)S(1)}, s32[768]{0:T(1024)}, u32[]{:S(2)}) copy-start(s32[768]{0:T(1024)} %param.11) | copy-start | bytes 9220
  22.3 111.8 %all-to-all-start.1 = ((f32[8,192,768]{2,1,0:T(8,128)}), f32[8,192,768]{2,1,0:T(8,128)}, u32[]{:S(2)}, u32[]{:S(2)}) async-start(f32[8,192,768]{2,1,0:T(8,128)} %bitcast.91), calls=%async_computation.1 | async-start | bytes 9437184 | tf_op jit(solution)/shard_map/all_to_all | solution.py:79
  28.8 117.3 %copy-start.3 = (s32[768]{0:T(1024)S(1)}, s32[768]{0:T(1024)}, u32[]{:S(2)}) copy-start(s32[768]{0:T(1024)} %param.13) | copy-start | bytes 9220
  28.8 209.0 %reduce-scatter.2.cloned.1.call-start = ((), (), s32[]{:S(2)}) async-start(), calls=%async_computation.4 | async-start | bytes 442368 | tf_op jit(solution)/shard_map/reduce_scatter | solution.py:119
  134.1 156.3 %collective-permute-start.1 = (f32[1536,768]{1,0:T(8,128)}, f32[1536,768]{1,0:T(8,128)}, u32[]{:S(2)}, u32[]{:S(2)}) collective-permute-start(f32[1536,768]{1,0:T(8,128)} %bitcast.6), channel_id=1, source_target_pairs={{0,24},{8,0},{16,8},{24,16},{1,25},{9,1},{17,9},{25,17},{2,26},{10... | collective-permute-start | bytes 14155784 | tf_op jit(solution)/shard_map/ppermute | solution.py:13
  142.7 8.9 %all-to-all-start = ((s32[8,1,192]{2,1,0:T(1,128)}), s32[8,1,192]{2,1,0:T(1,128)S(1)}, u32[]{:S(2)}, u32[]{:S(2)}) async-start(s32[8,1,192]{2,1,0:T(1,128)} %all_to_all.17), calls=%async_computation | async-start | bytes 16384 | tf_op jit(solution)/shard_map/all_to_all | solution.py:86
  151.7 86.1 %collective-permute-start = (s32[1536]{0:T(1024)S(1)}, s32[1536]{0:T(1024)S(1)}, u32[]{:S(2)}, u32[]{:S(2)}) collective-permute-start(s32[1536]{0:T(1024)S(1)} %reshape.144), channel_id=1, source_target_pairs={{0,24},{8,0},{16,8},{24,16},{1,25},{9,1},{17,9},{25,17},{2,26},{10... | collective-permute-start | bytes 18440 | tf_op jit(solution)/shard_map/ppermute | solution.py:13
  152.2 85.6 %collective-permute-start.3 = (s32[1536]{0:T(1024)S(1)}, s32[1536]{0:T(1024)S(1)}, u32[]{:S(2)}, u32[]{:S(2)}) collective-permute-start(s32[1536]{0:T(1024)S(1)} %reshape.144), channel_id=1, source_target_pairs={{0,16},{8,24},{16,0},{24,8},{1,17},{9,25},{17,1},{25,9},{2,18},{10... | collective-permute-start | bytes 18440 | tf_op jit(solution)/shard_map/ppermute | solution.py:13
  152.8 104.2 %copy-start.1 = (s32[8,1,192]{2,0,1:T(8,128)}, s32[8,1,192]{2,0,1:T(8,128)S(1)}, u32[]{:S(2)}) copy-start(s32[8,1,192]{2,0,1:T(8,128)S(1)} %copy.16) | copy-start | bytes 18436
  256.4 99.3 %collective-permute-start.4 = (f32[1536,768]{1,0:T(8,128)}, f32[1536,768]{1,0:T(8,128)}, u32[]{:S(2)}, u32[]{:S(2)}) collective-permute-start(f32[1536,768]{1,0:T(8,128)} %bitcast.6), channel_id=1, source_target_pairs={{0,16},{8,24},{16,0},{24,8},{1,17},{9,25},{17,1},{25,9},{2,18},{10... | collective-permute-start | bytes 14155784 | tf_op jit(solution)/shard_map/ppermute | solution.py:13
  323.3 65.3 %collective-permute-start.2 = (f32[1536]{0:T(1024)S(1)}, f32[1536]{0:T(1024)S(1)}, u32[]{:S(2)}, u32[]{:S(2)}) collective-permute-start(f32[1536]{0:T(1024)S(1)} %reshape.147), channel_id=1, source_target_pairs={{0,8},{8,16},{16,24},{24,0},{1,9},{9,17},{17,25},{25,1},{2,10},{10... | collective-permute-start | bytes 18440 | tf_op jit(solution)/shard_map/ppermute | solution.py:13
  389.4 9.0 %all-to-all-start.2 = ((f32[8,1,192]{2,1,0:T(1,128)}), f32[8,1,192]{2,1,0:T(1,128)S(1)}, u32[]{:S(2)}, u32[]{:S(2)}) async-start(f32[8,1,192]{2,1,0:T(1,128)} %all_to_all.21), calls=%async_computation.2 | async-start | bytes 16384 | tf_op jit(solution)/shard_map/all_to_all | solution.py:101
Sparse Core Ops, SparseCore 0:
  138.8 28.2 reduce-scatter.1
where the time goes:
time: 414 us
  waiting for transfers between devices  232 us (56%)
  matrix products  100 us (24%)
  blocking collectives  18.5 us (4%)
  starting transfers between devices  17.5 us (4%)
  other arithmetic  16.1 us (4%)
  between operations  14.3 us (3%)
  local copies, waits for them, and re-layouts  14.2 us (3%)
    ppermute x5, waiting for transfers between devices, passed_along(): return lax.ppermute(value, axis, pairs)  117 us
    all_to_all x1, waiting for transfers between devices, local(): lax.all_to_all(send_rows.reshape(owner_count, capacity, feature_width), '...  105 us
    dot_general x9, matrix products, masked_weights(): jnp.einsum('id,jd->ij', left_rows, right_rows, preferred_element_type=jnp...  98.5 us
    psum x1, blocking collectives, local(): cluster_sums = lax.psum(partial_value, 'grp')  18.5 us
    scatter x1, other arithmetic, local(): jnp.zeros((slot_count, feature_width), jnp.float32).at[slot_index]  9.76 us
  transfers between devices with their start and end apart: 9, of which 5 were waited for; matrix products, arithmetic and copies ran while one was open for 26% of the time, Pallas kernels for 0%

commit v1 on v0

--- a/solution.py
+++ b/solution.py
@@ -5,6 +5,29 @@
 
 CL_OWN = 16
 sharpness = 6.0
+
+
+def cut_along(value, dim, length):
+    before, after = (value.shape[:dim], value.shape[dim + 1 :])
+    return jnp.moveaxis(value.reshape(*before, length, -1, *after), dim, 0)
+
+
+def laid_out(blocks, dim):
+    blocks = jnp.moveaxis(blocks, 0, dim)
+    dims = blocks.shape
+    return blocks.reshape(*dims[:dim], dims[dim] * dims[dim + 1], *dims[dim + 2 :])
+
+
+def sent_to_each(shard, axis, split_dim, concat_dim):
+    size, index = (lax.axis_size(axis), lax.axis_index(axis))
+    parts = cut_along(shard, split_dim, size)
+    out = parts
+    for step in range(1, size):
+        target, source = ((index + step) % size, (index - step) % size)
+        sent = lax.dynamic_index_in_dim(parts, target, 0)
+        partner_block = lax.ppermute(sent, axis, [(i, (i + step) % size) for i in range(size)])
+        out = lax.dynamic_update_slice_in_dim(out, partner_block, source, axis=0)
+    return laid_out(out, concat_dim)
 
 
 def passed_along(value, axis, steps):
@@ -76,13 +99,7 @@
     send_rows = jnp.zeros((slot_count, feature_width), jnp.float32).at[slot_index].set(unit_embed)
     send_ids = jnp.full((slot_count,), -1, jnp.int32).at[slot_index].set(cluster_ids)
     held_rows, held_ids = (
-        lax.all_to_all(
-            send_rows.reshape(owner_count, capacity, feature_width),
-            "own",
-            split_axis=0,
-            concat_axis=0,
-            tiled=True,
-        ),
+        sent_to_each(send_rows.reshape(owner_count, capacity, feature_width), "own", 0, 0),
         lax.all_to_all(
             send_ids.reshape(owner_count, capacity), "own", split_axis=0, concat_axis=0, tiled=True
         ),

time: 414 us -> 418 us (level)
  waiting for transfers between devices: 232 us -> 159 us
  starting transfers between devices: 17.5 us -> 73.8 us
  local copies, waits for them, and re-layouts: 14.2 us -> 28.5 us
  blocking collectives: 18.5 us -> 24.8 us
    all_to_all x1 -> x0, waiting for transfers between devices: 105 us -> none  [local(): lax.all_to_all(send_rows.reshape(owner_count, capacity, feature_width), '...]
    ppermute x0 -> x7, waiting for transfers between devices: none -> 65.6 us  [sent_to_each(): lax.ppermute(sent, axis, [(i, (i + step) % size) for i in range(size)])]
    ppermute x5, waiting for transfers between devices: 117 us -> 83.2 us  [passed_along(): return lax.ppermute(value, axis, pairs)]
    all_to_all x1, starting transfers between devices: 3.33 us -> 32.9 us  [local(): lax.all_to_all(send_ids.reshape(owner_count, capacity), 'own', split_axis...]
    all_to_all x1, starting transfers between devices: 3.36 us -> 29.4 us  [local(): lax.all_to_all(dup_mass.reshape(owner_count, capacity), 'own', split_axis...]
    dynamic_update_slice x0 -> x6, local copies, waits for them, and re-layouts: none -> 9.46 us  [sent_to_each(): out = lax.dynamic_update_slice_in_dim(out, partner_block, source, axis=0)]
    ppermute x0 -> x7, starting transfers between devices: none -> 7.14 us  [sent_to_each(): lax.ppermute(sent, axis, [(i, (i + step) % size) for i in range(size)])]
    all_to_all x1 -> x0, starting transfers between devices: 6.49 us -> none  [local(): lax.all_to_all(send_rows.reshape(owner_count, capacity, feature_width), '...]
  transfers between devices with their start and end apart: 9 -> 15, of which waited for: 5 -> 8; matrix products, arithmetic and copies ran while one was open for 26% -> 27% of each run, Pallas kernels for 0% -> 0%
where the time goes in v1:
time: 418 us
  waiting for transfers between devices  159 us (38%)
  matrix products  100 us (24%)
  starting transfers between devices  73.8 us (18%)
  local copies, waits for them, and re-layouts  28.5 us (7%)
  blocking collectives  24.8 us (6%)
  other arithmetic  16.1 us (4%)
  between operations  14.3 us (3%)
    dot_general x9, matrix products, masked_weights(): jnp.einsum('id,jd->ij', left_rows, right_rows, preferred_element_type=jnp...  98.4 us
    ppermute x5, waiting for transfers between devices, passed_along(): return lax.ppermute(value, axis, pairs)  83.2 us
    ppermute x7, waiting for transfers between devices, sent_to_each(): lax.ppermute(sent, axis, [(i, (i + step) % size) for i in range(size)])  65.6 us
    all_to_all x1, starting transfers between devices, local(): lax.all_to_all(send_ids.reshape(owner_count, capacity), 'own', split_axis...  32.9 us
    all_to_all x1, starting transfers between devices, local(): lax.all_to_all(dup_mass.reshape(owner_count, capacity), 'own', split_axis...  29.4 us
    psum x1, blocking collectives, local(): cluster_sums = lax.psum(partial_value, 'grp')  24.8 us
    scatter x1, other arithmetic, local(): jnp.zeros((slot_count, feature_width), jnp.float32).at[slot_index]  9.83 us
    dynamic_update_slice x6, local copies, waits for them, and re-layouts, sent_to_each(): out = lax.dynamic_update_slice_in_dim(out, partner_block, source, axis=0)  9.46 us
  transfers between devices with their start and end apart: 15, of which 8 were waited for; matrix products, arithmetic and copies ran while one was open for 27% of the time, Pallas kernels for 0%

profile of v1, /device:TPU:0, one launch (start us, length us, event | category | flops | bytes accessed | tf_op | source)
XLA Modules:
  0.0 417.6 jit_solution(9799029502894822161)
XLA Ops:
  12.6 9.8 %scatter_custom_fusion.1 = f32[1536,768]{1,0:T(8,128)} fusion(s32[768]{0:T(1024)S(1)} %fusion.42, f32[]{:T(128)} %constant.217.clone.1, f32[768,768]{1,0:T(8,128)S(1)} %copy-done, f32[768]{0:T(1024)S(1)} %add_rsqrt_fusion), kind=kCustom, calls=%fused_computation.40 | custom fusion | flops 589824 | bytes 7081988 | tf_op jit(solution)/shard_map/scatter | solution.py:99
  24.1 11.7 %collective-permute-done = f32[1,1,192,768]{3,2,0,1:T(8,128)} collective-permute-done((f32[1,1,192,768]{3,2,0,1:T(8,128)S(1)}, f32[1,1,192,768]{3,2,0,1:T(8,128)}, u32[]{:S(2)}, u32[]{:S(2)}) %collective-permute-start) | collective-permute-done | bytes 589856 | tf_op jit(solution)/shard_map/ppermute | solution.py:28
  35.8 3.7 constant_dynamic-slice_fusion.3
  39.9 2.6 collective-permute-start.3
  42.4 2.4 collective-permute-start.4
  46.3 11.7 %collective-permute-done.1 = f32[1,1,192,768]{3,2,0,1:T(8,128)} collective-permute-done((f32[1,1,192,768]{3,2,0,1:T(8,128)}, f32[1,1,192,768]{3,2,0,1:T(8,128)}, u32[]{:S(2)}, u32[]{:S(2)}) %collective-permute-start.1) | collective-permute-done | bytes 589856 | tf_op jit(solution)/shard_map/ppermute | solution.py:28
  58.0 2.0 constant_dynamic-update-slice_fusion.5
  60.0 39.0 %collective-permute-done.2 = f32[1,1,192,768]{3,2,0,1:T(8,128)} collective-permute-done((f32[1,1,192,768]{3,2,0,1:T(8,128)}, f32[1,1,192,768]{3,2,0,1:T(8,128)}, u32[]{:S(2)}, u32[]{:S(2)}) %collective-permute-start.2) | collective-permute-done | bytes 589856 | tf_op jit(solution)/shard_map/ppermute | solution.py:28
  105.6 3.3 collective-permute-done.6
  109.7 2.4 collective-permute-start.8
  114.3 3.4 scatter_custom_fusion
  118.3 32.9 %all-to-all-start = ((s32[8,1,192]{2,1,0:T(1,128)}), s32[8,1,192]{2,1,0:T(1,128)S(1)}, u32[]{:S(2)}, u32[]{:S(2)}) async-start(s32[8,1,192]{2,1,0:T(1,128)} %all_to_all.14), calls=%async_computation | async-start | bytes 16384 | tf_op jit(solution)/shard_map/all_to_all | solution.py:103
  151.3 5.6 %all-to-all-done = s32[8,1,192]{2,1,0:T(1,128)S(1)} async-done(((s32[8,1,192]{2,1,0:T(1,128)}), s32[8,1,192]{2,1,0:T(1,128)S(1)}, u32[]{:S(2)}, u32[]{:S(2)}) %all-to-all-start) | async-done | bytes 6176 | tf_op jit(solution)/shard_map/all_to_all | solution.py:103
  158.3 50.1 %collective-permute-done.7 = s32[1536]{0:T(1024)S(1)} collective-permute-done((s32[1536]{0:T(1024)S(1)}, s32[1536]{0:T(1024)S(1)}, u32[]{:S(2)}, u32[]{:S(2)}) %collective-permute-start.7) | collective-permute-done | bytes 6176 | tf_op jit(solution)/shard_map/ppermute | solution.py:36
  208.5 24.8 %psum.7 = f32[16,768]{1,0:T(8,128)S(1)} all-reduce(f32[16,768]{1,0:T(8,128)} %reduce-scatter.2.cloned.1.call-done), channel_id=1, replica_groups=mesh['grp'=4,'own'=8] {'grp'}, use_global_device_ids=true, to_apply=%region_21.22 | all-reduce | flops 12288 | bytes 98304 | tf_op jit(solution)/shard_map/psum | solution.py:137
  234.0 33.4 %while.44 = (s32[]{:T(128)}, f32[1536]{0:T(1024)S(1)}, s32[8,192]{1,0:T(8,128)}, s32[3,512]{1,0:T(4,128)S(1)}, f32[3,512,768]{2,1,0:T(8,128)}, /*index=5*/f32[15...) while((s32[]{:T(128)}, f32[1536]{0:T(1024)S(1)}, s32[8,192]{1,0:T(8,128)}, ...), condition=%wide.wide.region_9.10_spmd.clone, body=%wide.wide.region_7.9_spmd.clone.sunk | while | flops 7252478976 | bytes 6338155 | solution.py:76
  234.0 11.4 %fusion.67 = f32[1536]{0:T(1024)S(1)} fusion(f32[1536,768]{1,0:T(8,128)} %get-tuple-element.660, f32[3,512,768]{2,1,0:T(8,128)} %bitcast.97, s32[]{:T(128)} %get-tuple-element.646, pred[1536]{0:T(1024)(128)(4,1)S(1)} %broadcast_compare_fusion.9, s32[512]{0:T(512)S(1)} %bitcast.106, s32[1536]{0:T(1024)S(1)} %get-tuple-element.661), kind=kOutput, calls=%fused_computation.11.clone.clone.1 | convolution fusion | flops 7252474368 | bytes 6307840 | tf_op jit(solution)/shard_map/while/body/eval_jaxpr/id,jd->ij/dot_general | solution.py:53
  245.5 10.9 %fusion.67 = f32[1536]{0:T(1024)S(1)} fusion(f32[1536,768]{1,0:T(8,128)} %get-tuple-element.660, f32[3,512,768]{2,1,0:T(8,128)} %bitcast.97, s32[]{:T(128)} %get-tuple-element.646, pred[1536]{0:T(1024)(128)(4,1)S(1)} %broadcast_compare_fusion.9, s32[512]{0:T(512)S(1)} %bitcast.106, s32[1536]{0:T(1024)S(1)} %get-tuple-element.661), kind=kOutput, calls=%fused_computation.11.clone.clone.1 | convolution fusion | flops 7252474368 | bytes 6307840 | tf_op jit(solution)/shard_map/while/body/eval_jaxpr/id,jd->ij/dot_general | solution.py:53
  256.5 10.9 %fusion.67 = f32[1536]{0:T(1024)S(1)} fusion(f32[1536,768]{1,0:T(8,128)} %get-tuple-element.660, f32[3,512,768]{2,1,0:T(8,128)} %bitcast.97, s32[]{:T(128)} %get-tuple-element.646, pred[1536]{0:T(1024)(128)(4,1)S(1)} %broadcast_compare_fusion.9, s32[512]{0:T(512)S(1)} %bitcast.106, s32[1536]{0:T(1024)S(1)} %get-tuple-element.661), kind=kOutput, calls=%fused_computation.11.clone.clone.1 | convolution fusion | flops 7252474368 | bytes 6307840 | tf_op jit(solution)/shard_map/while/body/eval_jaxpr/id,jd->ij/dot_general | solution.py:53
  267.4 32.8 %while.45 = (s32[]{:T(128)}, f32[1536]{0:T(1024)S(1)}, f32[3,512]{1,0:T(4,128)S(1)}, s32[8,192]{1,0:T(8,128)}, s32[3,512]{1,0:T(4,128)S(1)}, /*index=5*/f32[3,51...) while((s32[]{:T(128)}, f32[1536]{0:T(1024)S(1)}, ...), condition=%wide.wide.region_13.14_spmd.clone, body=%wide.wide.region_10.13_spmd.clone.sunk | while | flops 7253264896 | bytes 6344311 | solution.py:76
  267.5 10.8 %fusion.69 = (f32[512]{0:T(512)S(1)}, f32[1536]{0:T(1024)S(1)}) fusion(f32[1536,768]{1,0:T(8,128)} %get-tuple-element.633, f32[3,512,768]{2,1,0:T(8,128)} %get-tuple-element.632, s32[]{:T(128)} %get-tuple-element.617, pred[1536]{0:T(1024)(128)(4,1)S(1)} %broadcast_compare_fusion.10, s32[512]{0:T(512)S(1)} %bitcast.105, ...), kind=kOutput, calls=%fused_computation.92.clone.clone.1 | convolution fusion | flops 7253260288 | bytes 6309888 | tf_op jit(solution)/shard_map/while/body/eval_jaxpr/id,jd->ij/dot_general | solution.py:53
  278.4 10.8 %fusion.69 = (f32[512]{0:T(512)S(1)}, f32[1536]{0:T(1024)S(1)}) fusion(f32[1536,768]{1,0:T(8,128)} %get-tuple-element.633, f32[3,512,768]{2,1,0:T(8,128)} %get-tuple-element.632, s32[]{:T(128)} %get-tuple-element.617, pred[1536]{0:T(1024)(128)(4,1)S(1)} %broadcast_compare_fusion.10, s32[512]{0:T(512)S(1)} %bitcast.105, ...), kind=kOutput, calls=%fused_computation.92.clone.clone.1 | convolution fusion | flops 7253260288 | bytes 6309888 | tf_op jit(solution)/shard_map/while/body/eval_jaxpr/id,jd->ij/dot_general | solution.py:53
  289.3 10.8 %fusion.69 = (f32[512]{0:T(512)S(1)}, f32[1536]{0:T(1024)S(1)}) fusion(f32[1536,768]{1,0:T(8,128)} %get-tuple-element.633, f32[3,512,768]{2,1,0:T(8,128)} %get-tuple-element.632, s32[]{:T(128)} %get-tuple-element.617, pred[1536]{0:T(1024)(128)(4,1)S(1)} %broadcast_compare_fusion.10, s32[512]{0:T(512)S(1)} %bitcast.105, ...), kind=kOutput, calls=%fused_computation.92.clone.clone.1 | convolution fusion | flops 7253260288 | bytes 6309888 | tf_op jit(solution)/shard_map/while/body/eval_jaxpr/id,jd->ij/dot_general | solution.py:53
  300.5 33.1 %collective-permute-done.11 = f32[1536,768]{1,0:T(8,128)} collective-permute-done((f32[1536,768]{1,0:T(8,128)}, f32[1536,768]{1,0:T(8,128)}, u32[]{:S(2)}, u32[]{:S(2)}) %collective-permute-start.11) | collective-permute-done | bytes 4718624 | tf_op jit(solution)/shard_map/ppermute | solution.py:36
  333.6 32.9 %while.46 = (s32[]{:T(128)}, f32[1536]{0:T(1024)S(1)}, s32[8,192]{1,0:T(8,128)}, s32[3,512]{1,0:T(4,128)S(1)}, f32[3,512,768]{2,1,0:T(8,128)}, /*index=5*/f32[15...) while((s32[]{:T(128)}, f32[1536]{0:T(1024)S(1)}, s32[8,192]{1,0:T(8,128)}, ...), condition=%wide.wide.region_16.17_spmd.clone, body=%wide.wide.region_14.16_spmd.clone.sunk | while | flops 7252478976 | bytes 6338155 | solution.py:76
  333.6 10.9 %fusion.72 = f32[1536]{0:T(1024)S(1)} fusion(f32[1536,768]{1,0:T(8,128)} %get-tuple-element.603, f32[3,512,768]{2,1,0:T(8,128)} %get-tuple-element.602, s32[]{:T(128)} %get-tuple-element.589, pred[1536]{0:T(1024)(128)(4,1)S(1)} %broadcast_compare_fusion.11, s32[512]{0:T(512)S(1)} %bitcast.107, s32[1536]{0:T(1024)S(1)} %get-tuple-element.604), kind=kOutput, calls=%fused_computation.34.clone.clone.1 | convolution fusion | flops 7252474368 | bytes 6307840 | tf_op jit(solution)/shard_map/while/body/eval_jaxpr/id,jd->ij/dot_general | solution.py:53
  344.6 10.9 %fusion.72 = f32[1536]{0:T(1024)S(1)} fusion(f32[1536,768]{1,0:T(8,128)} %get-tuple-element.603, f32[3,512,768]{2,1,0:T(8,128)} %get-tuple-element.602, s32[]{:T(128)} %get-tuple-element.589, pred[1536]{0:T(1024)(128)(4,1)S(1)} %broadcast_compare_fusion.11, s32[512]{0:T(512)S(1)} %bitcast.107, s32[1536]{0:T(1024)S(1)} %get-tuple-element.604), kind=kOutput, calls=%fused_computation.34.clone.clone.1 | convolution fusion | flops 7252474368 | bytes 6307840 | tf_op jit(solution)/shard_map/while/body/eval_jaxpr/id,jd->ij/dot_general | solution.py:53
  355.6 10.9 %fusion.72 = f32[1536]{0:T(1024)S(1)} fusion(f32[1536,768]{1,0:T(8,128)} %get-tuple-element.603, f32[3,512,768]{2,1,0:T(8,128)} %get-tuple-element.602, s32[]{:T(128)} %get-tuple-element.589, pred[1536]{0:T(1024)(128)(4,1)S(1)} %broadcast_compare_fusion.11, s32[512]{0:T(512)S(1)} %bitcast.107, s32[1536]{0:T(1024)S(1)} %get-tuple-element.604), kind=kOutput, calls=%fused_computation.34.clone.clone.1 | convolution fusion | flops 7252474368 | bytes 6307840 | tf_op jit(solution)/shard_map/while/body/eval_jaxpr/id,jd->ij/dot_general | solution.py:53
  367.2 29.4 %all-to-all-start.1 = ((f32[8,1,192]{2,1,0:T(1,128)}), f32[8,1,192]{2,1,0:T(1,128)S(1)}, u32[]{:S(2)}, u32[]{:S(2)}) async-start(f32[8,1,192]{2,1,0:T(1,128)} %all_to_all.17), calls=%async_computation.1 | async-start | bytes 16384 | tf_op jit(solution)/shard_map/all_to_all | solution.py:118
  397.3 4.9 %all-to-all-done.1 = f32[8,1,192]{2,1,0:T(1,128)S(1)} async-done(((f32[8,1,192]{2,1,0:T(1,128)}), f32[8,1,192]{2,1,0:T(1,128)S(1)}, u32[]{:S(2)}, u32[]{:S(2)}) %all-to-all-start.1) | async-done | bytes 6176 | tf_op jit(solution)/shard_map/all_to_all | solution.py:118
  402.3 4.5 %gather_fusion = f32[768]{0:T(1024)S(1)} fusion(f32[1536]{0:T(1024)S(1)} %reshape.142, s32[1024]{0:T(1024)S(1)} %pad_clamp_fusion), kind=kCustom, calls=%fused_computation | custom fusion | bytes 9216 | tf_op jit(solution)/shard_map/gather | solution.py:121
  406.8 3.9 scatter_custom_fusion.2
  (107 shorter events, 23.3 us)
Async XLA Ops:
  7.2 5.4 %copy-start = (f32[768,768]{1,0:T(8,128)S(1)}, f32[768,768]{1,0:T(8,128)}, u32[]{:S(2)}) copy-start(f32[768,768]{1,0:T(8,128)} %param.10) | copy-start | bytes 7077892
  7.2 201.3 %reduce-scatter.2.cloned.1.call-start = ((), (), s32[]{:S(2)}) async-start(), calls=%async_computation.3 | async-start | bytes 442368 | tf_op jit(solution)/shard_map/reduce_scatter | solution.py:136
  23.6 12.2 %collective-permute-start = (f32[1,1,192,768]{3,2,0,1:T(8,128)S(1)}, f32[1,1,192,768]{3,2,0,1:T(8,128)}, u32[]{:S(2)}, u32[]{:S(2)}) collective-permute-start(f32[1,1,192,768]{3,2,0,1:T(8,128)S(1)} %constant_dynamic-slice_fusion.9), channel_id=1, source_target_pairs={{0,1},{1,2},{2,3},{3,4},{4,5},{5,6},{6,7},{7,0},{8,9},{9,10},{10,1... | collective-permute-start | bytes 1769480 | tf_op jit(solution)/shard_map/ppermute | solution.py:28
  24.1 22.0 %copy-start.4 = (s32[128]{0:T(128)S(1)}, s32[128]{0:T(128)}, u32[]{:S(2)}) copy-start(s32[128]{0:T(128)} %param.12) | copy-start | bytes 1540
  39.5 18.5 %collective-permute-start.1 = (f32[1,1,192,768]{3,2,0,1:T(8,128)}, f32[1,1,192,768]{3,2,0,1:T(8,128)}, u32[]{:S(2)}, u32[]{:S(2)}) collective-permute-start(f32[1,1,192,768]{3,2,0,1:T(8,128)} %get-tuple-element.361), channel_id=1, source_target_pairs={{0,2},{1,3},{2,4},{3,5},{4,6},{5,7},{6,0},{7,1},{8,10},{9,11},{10,... | collective-permute-start | bytes 1769480 | tf_op jit(solution)/shard_map/ppermute | solution.py:28
  39.8 59.1 %collective-permute-start.2 = (f32[1,1,192,768]{3,2,0,1:T(8,128)}, f32[1,1,192,768]{3,2,0,1:T(8,128)}, u32[]{:S(2)}, u32[]{:S(2)}) collective-permute-start(f32[1,1,192,768]{3,2,0,1:T(8,128)} %get-tuple-element.360), channel_id=1, source_target_pairs={{0,3},{1,4},{2,5},{3,6},{4,7},{5,0},{6,1},{7,2},{8,11},{9,12},{10,... | collective-permute-start | bytes 1769480 | tf_op jit(solution)/shard_map/ppermute | solution.py:28
  39.9 61.0 %collective-permute-start.3 = (f32[1,1,192,768]{3,2,0,1:T(8,128)}, f32[1,1,192,768]{3,2,0,1:T(8,128)}, u32[]{:S(2)}, u32[]{:S(2)}) collective-permute-start(f32[1,1,192,768]{3,2,0,1:T(8,128)} %get-tuple-element.359), channel_id=1, source_target_pairs={{0,4},{1,5},{2,6},{3,7},{4,0},{5,1},{6,2},{7,3},{8,12},{9,13},{10,... | collective-permute-start | bytes 1769480 | tf_op jit(solution)/shard_map/ppermute | solution.py:28
  42.4 60.4 %collective-permute-start.4 = (f32[1,1,192,768]{3,2,0,1:T(8,128)}, f32[1,1,192,768]{3,2,0,1:T(8,128)}, u32[]{:S(2)}, u32[]{:S(2)}) collective-permute-start(f32[1,1,192,768]{3,2,0,1:T(8,128)} %get-tuple-element.358), channel_id=1, source_target_pairs={{0,5},{1,6},{2,7},{3,0},{4,1},{5,2},{6,3},{7,4},{8,13},{9,14},{10,... | collective-permute-start | bytes 1769480 | tf_op jit(solution)/shard_map/ppermute | solution.py:28
  44.8 59.9 %collective-permute-start.5 = (f32[1,1,192,768]{3,2,0,1:T(8,128)S(1)}, f32[1,1,192,768]{3,2,0,1:T(8,128)S(1)}, u32[]{:S(2)}, u32[]{:S(2)}) collective-permute-start(f32[1,1,192,768]{3,2,0,1:T(8,128)S(1)} %get-tuple-element.357), channel_id=1, source_target_pairs={{0,6},{1,7},{2,0},{3,1},{4,2},{5,3},{6,4},{7,5},{8,14},{9,15},{10,... | collective-permute-start | bytes 1769480 | tf_op jit(solution)/shard_map/ppermute | solution.py:28
  58.0 50.9 %collective-permute-start.6 = (f32[1,1,192,768]{3,2,0,1:T(8,128)S(1)}, f32[1,1,192,768]{3,2,0,1:T(8,128)S(1)}, u32[]{:S(2)}, u32[]{:S(2)}) collective-permute-start(f32[1,1,192,768]{3,2,0,1:T(8,128)S(1)} %get-tuple-element.356), channel_id=1, source_target_pairs={{0,7},{1,0},{2,1},{3,2},{4,3},{5,4},{6,5},{7,6},{8,15},{9,8},{10,9... | collective-permute-start | bytes 1769480 | tf_op jit(solution)/shard_map/ppermute | solution.py:28
  60.0 52.2 %copy-start.5 = (s32[128]{0:T(128)S(1)}, s32[128]{0:T(128)}, u32[]{:S(2)}) copy-start(s32[128]{0:T(128)} %param.12) | copy-start | bytes 1540
  60.0 52.3 %copy-start.2 = (s32[768]{0:T(1024)S(1)}, s32[768]{0:T(1024)}, u32[]{:S(2)}) copy-start(s32[768]{0:T(1024)} %param.11) | copy-start | bytes 9220
  102.8 48.4 %copy-start.3 = (s32[768]{0:T(1024)S(1)}, s32[768]{0:T(1024)}, u32[]{:S(2)}) copy-start(s32[768]{0:T(1024)} %param.13) | copy-start | bytes 9220
  109.7 157.7 %collective-permute-start.8 = (f32[1536,768]{1,0:T(8,128)}, f32[1536,768]{1,0:T(8,128)}, u32[]{:S(2)}, u32[]{:S(2)}) collective-permute-start(f32[1536,768]{1,0:T(8,128)} %bitcast.93), channel_id=1, source_target_pairs={{0,24},{8,0},{16,8},{24,16},{1,25},{9,1},{17,9},{25,17},{2,26},{10... | collective-permute-start | bytes 14155784 | tf_op jit(solution)/shard_map/ppermute | solution.py:36
  118.3 38.5 %all-to-all-start = ((s32[8,1,192]{2,1,0:T(1,128)}), s32[8,1,192]{2,1,0:T(1,128)S(1)}, u32[]{:S(2)}, u32[]{:S(2)}) async-start(s32[8,1,192]{2,1,0:T(1,128)} %all_to_all.14), calls=%async_computation | async-start | bytes 16384 | tf_op jit(solution)/shard_map/all_to_all | solution.py:103
  156.9 51.5 %collective-permute-start.7 = (s32[1536]{0:T(1024)S(1)}, s32[1536]{0:T(1024)S(1)}, u32[]{:S(2)}, u32[]{:S(2)}) collective-permute-start(s32[1536]{0:T(1024)S(1)} %reshape.136), channel_id=1, source_target_pairs={{0,24},{8,0},{16,8},{24,16},{1,25},{9,1},{17,9},{25,17},{2,26},{10... | collective-permute-start | bytes 18440 | tf_op jit(solution)/shard_map/ppermute | solution.py:36
  157.5 51.0 %collective-permute-start.10 = (s32[1536]{0:T(1024)S(1)}, s32[1536]{0:T(1024)S(1)}, u32[]{:S(2)}, u32[]{:S(2)}) collective-permute-start(s32[1536]{0:T(1024)S(1)} %reshape.136), channel_id=1, source_target_pairs={{0,16},{8,24},{16,0},{24,8},{1,17},{9,25},{17,1},{25,9},{2,18},{10... | collective-permute-start | bytes 18440 | tf_op jit(solution)/shard_map/ppermute | solution.py:36
  158.1 75.9 %copy-start.1 = (s32[8,1,192]{2,0,1:T(8,128)}, s32[8,1,192]{2,0,1:T(8,128)S(1)}, u32[]{:S(2)}) copy-start(s32[8,1,192]{2,0,1:T(8,128)S(1)} %copy.16) | copy-start | bytes 18436
  233.4 100.2 %collective-permute-start.11 = (f32[1536,768]{1,0:T(8,128)}, f32[1536,768]{1,0:T(8,128)}, u32[]{:S(2)}, u32[]{:S(2)}) collective-permute-start(f32[1536,768]{1,0:T(8,128)} %bitcast.94), channel_id=1, source_target_pairs={{0,16},{8,24},{16,0},{24,8},{1,17},{9,25},{17,1},{25,9},{2,18},{10... | collective-permute-start | bytes 14155784 | tf_op jit(solution)/shard_map/ppermute | solution.py:36
  300.2 66.3 %collective-permute-start.9 = (f32[1536]{0:T(1024)S(1)}, f32[1536]{0:T(1024)S(1)}, u32[]{:S(2)}, u32[]{:S(2)}) collective-permute-start(f32[1536]{0:T(1024)S(1)} %reshape.139), channel_id=1, source_target_pairs={{0,8},{8,16},{16,24},{24,0},{1,9},{9,17},{17,25},{25,1},{2,10},{10... | collective-permute-start | bytes 18440 | tf_op jit(solution)/shard_map/ppermute | solution.py:36
  367.2 35.0 %all-to-all-start.1 = ((f32[8,1,192]{2,1,0:T(1,128)}), f32[8,1,192]{2,1,0:T(1,128)S(1)}, u32[]{:S(2)}, u32[]{:S(2)}) async-start(f32[8,1,192]{2,1,0:T(1,128)} %all_to_all.17), calls=%async_computation.1 | async-start | bytes 16384 | tf_op jit(solution)/shard_map/all_to_all | solution.py:118
Sparse Core Ops, SparseCore 0:
  114.4 58.5 reduce-scatter.1
